TPU v7x, 32 devices: a whole 2x2x4 slice. The times are simulated.
32 devices in a mesh: pts: 8 (over y, x, core), val: 4 (over z).
Axes of the slice: x: 2, y: 2, z: 4, core: 2. Of those that a mesh axis runs over, the one named last changes fastest.
Arguments:
- vectors: float32 [1, 512, 2048], P(None, 'val', 'pts'), may hold values from -6 to 6
- eval_energy: float32 [512], P('val'), may hold values from -2 to -0.2
- cond_energy: float32 [2048], P('pts'), may hold values from 0.2 to 2
- val_orbitals: float32 [512, 8192], P('pts', 'val'), may hold values from -0.25 to 0.25
- cond_orbitals: float32 [2048, 8192], P('val', 'pts'), may hold values from -0.125 to 0.125
- screened: float32 [8192, 8192], P('val', 'pts'), may hold values from -1.5 to 1.5
Outputs:
- filtered: float32 [1, 512, 2048], P(None, 'val', 'pts')
All inputs are finite; a program needn't handle non-finite values.
Results may differ from a plain program's by a relative error of at most 0.00013.
Values sent between devices are 32-bit elements; how exact they have to be, the bound alone decides.
A program may use at most 128 MiB of HBM per device.

v0:
```python
import jax
import jax.numpy as jnp
from jax import lax
from jax.sharding import PartitionSpec as P

ITERS = 2
CENTER = 2.2
HALF_WIDTH = 2.0


def per_device(vectors, eval_energy, cond_energy, val_orbitals, cond_orbitals, screened):
    highest = lax.Precision.HIGHEST
    cond_whole = lax.all_gather(cond_orbitals, "val", axis=0, tiled=True)
    val_whole = lax.all_gather(val_orbitals, "pts", axis=0, tiled=True)
    ediff = cond_energy[None, None, :] - eval_energy[None, :, None]
    older = vectors
    newer = vectors
    for step in range(ITERS):
        direct_full_x = lax.all_gather(newer, "pts", axis=2, tiled=True)
        pair = jnp.einsum(
            "bvc,cn->bvn",
            direct_full_x,
            cond_whole,
            precision=highest,
            preferred_element_type=jnp.float32,
        )
        pair_all = lax.all_gather(pair, "val", axis=1, tiled=True)
        mixed = jnp.einsum(
            "vm,bvn->bmn",
            val_whole,
            pair_all,
            precision=highest,
            preferred_element_type=jnp.float32,
        )
        weighted = mixed * screened[None, :, :]
        back_terms = jnp.einsum(
            "vm,bmn->bvn",
            val_whole,
            weighted,
            precision=highest,
            preferred_element_type=jnp.float32,
        )
        back = lax.psum_scatter(back_terms, "val", scatter_dimension=1, tiled=True)
        hamil = ediff * newer - lax.psum_scatter(
            jnp.einsum(
                "bvn,cn->bvc",
                back,
                cond_whole,
                precision=highest,
                preferred_element_type=jnp.float32,
            ),
            "pts",
            scatter_dimension=2,
            tiled=True,
        )
        scaled = (hamil - CENTER * newer) / HALF_WIDTH
        if step == 0:
            following = scaled
        else:
            following = 2.0 * scaled - older
        older = newer
        newer = following
    return newer


def solution(mesh):
    placed = (
        P(None, "val", "pts"),
        P("val"),
        P("pts"),
        P("pts", "val"),
        P("val", "pts"),
        P("val", "pts"),
    )
    return jax.shard_map(
        per_device, mesh=mesh, in_specs=placed, out_specs=P(None, "val", "pts"), check_vma=False
    )
```

profile of v0, /device:TPU:0, one launch (start us, length us, event | category | flops | bytes accessed | tf_op | source)
XLA Modules:
  0.0 608.8 jit_solution(13954029730441035257)
XLA Ops:
  6.5 0.0 all-gather.9.cloned.1.call-start
  6.5 0.7 all-gather.9.cloned.1.call-update
  7.3 0.0 all-gather.11.cloned.1.call-start
  7.3 0.7 all-gather.11.cloned.1.call-update
  8.0 0.0 all-gather.13.cloned.1.call-start
  8.1 0.7 all-gather.13.cloned.1.call-update
  8.7 0.0 all-gather.17.cloned.1.call-start
  8.8 26.7 %all-gather.9.cloned.1.call-done = f32[1,128,2048]{2,1,0:T(8,128)} async-done(((f32[1,128,256]{2,1,0:T(8,128)}), f32[1,128,2048]{2,1,0:T(8,128)}) %all-gather.9.cloned.1.call-update) | async-done | bytes 1048592 | tf_op jit(solution)/shard_map/all_gather | solution.py:19
  35.4 151.2 %all-gather.11.cloned.1.call-done = f32[2048,1024]{1,0:T(8,128)} async-done(((f32[512,1024]{1,0:T(8,128)}), f32[2048,1024]{1,0:T(8,128)}) %all-gather.11.cloned.1.call-update) | async-done | bytes 8388624 | tf_op jit(solution)/shard_map/all_gather | solution.py:13
  186.7 9.2 %fusion.16 = f32[128,1024]{1,0:T(8,128)} fusion(f32[2048,1024]{1,0:T(8,128)} %all-gather.11.cloned.1.call-done, f32[1,128,2048]{2,1,0:T(8,128)} %all-gather.9.cloned.1.call-done), kind=kOutput, calls=%fused_computation.14 | convolution fusion | flops 3221225472 | bytes 9961472 | tf_op jit(solution)/shard_map/bvc,cn->bvn/dot_general | solution.py:20
  195.8 0.0 all-gather.17.cloned.1.call-update
  195.8 0.2 reduce-scatter.5.cloned.1.call-start
  196.1 9.1 %copy.7 = f32[2048,1024]{0,1:T(8,128)} copy(f32[2048,1024]{1,0:T(8,128)} %param.11) | data formatting | bytes 16777216 | tf_op args[5]
  205.2 18.1 %all-gather.13.cloned.1.call-done = f32[512,2048]{1,0:T(8,128)} async-done(((f32[64,2048]{1,0:T(8,128)}), f32[512,2048]{1,0:T(8,128)}) %all-gather.13.cloned.1.call-update) | async-done | bytes 4194320 | tf_op jit(solution)/shard_map/all_gather | solution.py:14
  223.3 47.1 %all-gather.17.cloned.1.call-done = f32[512,1024]{1,0:T(8,128)} async-done(((f32[128,1024]{1,0:T(8,128)}), f32[512,1024]{1,0:T(8,128)}) %all-gather.17.cloned.1.call-update) | async-done | bytes 2097168 | tf_op jit(solution)/shard_map/all_gather | solution.py:27
  270.5 17.0 %fusion.26 = f32[1024,2048]{1,0:T(8,128)S(1)} fusion(f32[512,1024]{1,0:T(8,128)} %all-gather.17.cloned.1.call-done, f32[512,2048]{1,0:T(8,128)} %all-gather.13.cloned.1.call-done), kind=kOutput, calls=%fused_computation.26 | convolution fusion | flops 12884901888 | bytes 14680064 | tf_op jit(solution)/shard_map/vm,bvn->bmn/dot_general | solution.py:28
  287.4 0.0 copy-done
  287.4 0.0 copy-done.1
  287.5 15.3 %fusion.8 = f32[1,512,1024]{1,2,0:T(8,128)} fusion(f32[512,2048]{1,0:T(8,128)S(1)} %copy-done.1, f32[1024,2048]{1,0:T(8,128)S(1)} %fusion.26, f32[2048,1024]{0,1:T(8,128)S(1)} %copy-done), kind=kOutput, calls=%fused_computation.10 | convolution fusion | flops 12886999040 | bytes 23068672 | tf_op jit(solution)/shard_map/vm,bmn->bvn/dot_general | solution.py:36
  302.8 0.0 reduce-scatter.5.cloned.1.call-update
  302.8 0.3 reduce-scatter.7.cloned.1.call-start
  303.1 42.3 %reduce-scatter.5.cloned.1.call-done = f32[1,128,1024]{1,2,0:T(8,128)} async-done(((f32[1,512,1024]{1,2,0:T(8,128)}), f32[1,128,1024]{1,2,0:T(8,128)}) %reduce-scatter.5.cloned.1.call-update) | async-done | bytes 524304 | tf_op jit(solution)/shard_map/reduce_scatter | solution.py:43
  345.4 13.4 %convolution_bitcast_fusion.1 = f32[1,128,2048]{2,1,0:T(8,128)} fusion(f32[2048,1024]{1,0:T(8,128)} %all-gather.11.cloned.1.call-done, f32[1,128,1024]{1,2,0:T(8,128)} %reduce-scatter.5.cloned.1.call-done), kind=kOutput, calls=%fused_computation.9 | convolution fusion | flops 3221225472 | bytes 9961472 | tf_op jit(solution)/shard_map/bvn,cn->bvc/dot_general | solution.py:45
  358.8 0.0 reduce-scatter.7.cloned.1.call-update
  358.8 0.0 all-gather.15.cloned.1.call-start
  358.8 35.3 %reduce-scatter.7.cloned.1.call-done = f32[1,128,256]{2,1,0:T(8,128)} async-done(((f32[1,128,2048]{2,1,0:T(8,128)}), f32[1,128,256]{2,1,0:T(8,128)}) %reduce-scatter.7.cloned.1.call-update) | async-done | bytes 131088 | tf_op jit(solution)/shard_map/reduce_scatter | solution.py:44
  394.1 0.0 copy-done.3
  394.1 0.0 copy-done.5
  394.1 0.0 copy-done.6
  394.1 1.7 fusion.25
  395.8 0.0 all-gather.15.cloned.1.call-update
  395.8 0.0 all-gather.19.cloned.1.call-start
  395.8 23.6 %all-gather.15.cloned.1.call-done = f32[1,128,2048]{2,1,0:T(8,128)} async-done(((f32[1,128,256]{2,1,0:T(8,128)}), f32[1,128,2048]{2,1,0:T(8,128)}) %all-gather.15.cloned.1.call-update) | async-done | bytes 1048592 | tf_op jit(solution)/shard_map/all_gather | solution.py:19
  419.5 9.2 %fusion.14 = f32[128,1024]{1,0:T(8,128)} fusion(f32[2048,1024]{1,0:T(8,128)} %all-gather.11.cloned.1.call-done, f32[1,128,2048]{2,1,0:T(8,128)} %all-gather.15.cloned.1.call-done), kind=kOutput, calls=%fused_computation.12 | convolution fusion | flops 3221225472 | bytes 9961472 | tf_op jit(solution)/shard_map/bvc,cn->bvn/dot_general | solution.py:20
  428.6 0.0 all-gather.19.cloned.1.call-update
  428.7 0.4 reduce-scatter.9.cloned.1.call-start
  429.1 45.4 %all-gather.19.cloned.1.call-done = f32[512,1024]{1,0:T(8,128)} async-done(((f32[128,1024]{1,0:T(8,128)}), f32[512,1024]{1,0:T(8,128)}) %all-gather.19.cloned.1.call-update) | async-done | bytes 2097168 | tf_op jit(solution)/shard_map/all_gather | solution.py:27
  474.5 16.9 %fusion.27 = f32[1024,2048]{1,0:T(8,128)S(1)} fusion(f32[512,1024]{1,0:T(8,128)} %all-gather.19.cloned.1.call-done, f32[512,2048]{1,0:T(8,128)} %all-gather.13.cloned.1.call-done), kind=kOutput, calls=%fused_computation.27 | convolution fusion | flops 12884901888 | bytes 14680064 | tf_op jit(solution)/shard_map/vm,bvn->bmn/dot_general | solution.py:28
  491.4 0.0 copy-done.2
  491.4 17.3 %fusion.11 = f32[1,512,1024]{1,2,0:T(8,128)} fusion(f32[512,2048]{1,0:T(8,128)S(1)} %copy-done.2, f32[1024,2048]{1,0:T(8,128)S(1)} %fusion.27, f32[2048,1024]{0,1:T(8,128)} %copy.7), kind=kOutput, calls=%fused_computation.11 | convolution fusion | flops 12886999040 | bytes 23068672 | tf_op jit(solution)/shard_map/vm,bmn->bvn/dot_general | solution.py:36
  508.7 0.0 reduce-scatter.9.cloned.1.call-update
  508.7 0.2 reduce-scatter.11.cloned.1.call-start
  508.9 42.4 %reduce-scatter.9.cloned.1.call-done = f32[1,128,1024]{1,2,0:T(8,128)} async-done(((f32[1,512,1024]{1,2,0:T(8,128)}), f32[1,128,1024]{1,2,0:T(8,128)}) %reduce-scatter.9.cloned.1.call-update) | async-done | bytes 524304 | tf_op jit(solution)/shard_map/reduce_scatter | solution.py:43
  551.3 13.4 %convolution_bitcast_fusion = f32[1,128,2048]{2,1,0:T(8,128)} fusion(f32[2048,1024]{1,0:T(8,128)} %all-gather.11.cloned.1.call-done, f32[1,128,1024]{1,2,0:T(8,128)} %reduce-scatter.9.cloned.1.call-done), kind=kOutput, calls=%fused_computation.8 | convolution fusion | flops 3221225472 | bytes 9961472 | tf_op jit(solution)/shard_map/bvn,cn->bvc/dot_general | solution.py:45
  564.8 0.0 reduce-scatter.11.cloned.1.call-update
  564.8 35.3 %reduce-scatter.11.cloned.1.call-done = f32[1,128,256]{2,1,0:T(8,128)} async-done(((f32[1,128,2048]{2,1,0:T(8,128)}), f32[1,128,256]{2,1,0:T(8,128)}) %reduce-scatter.11.cloned.1.call-update) | async-done | bytes 131088 | tf_op jit(solution)/shard_map/reduce_scatter | solution.py:44
  600.1 0.0 copy-done.4
  600.1 1.7 fusion.24
  (7 shorter events, 0.0 us)
Async XLA Ops:
  6.5 28.9 %all-gather.9.cloned.1.call-start = ((), (), s32[]{:S(2)}) async-start(), calls=%async_computation.4 | async-start | bytes 1179648 | tf_op jit(solution)/shard_map/all_gather | solution.py:19
  7.3 179.4 %all-gather.11.cloned.1.call-start = ((), (), s32[]{:S(2)}) async-start(), calls=%async_computation.5 | async-start | bytes 10485760 | tf_op jit(solution)/shard_map/all_gather | solution.py:13
  8.0 215.3 %all-gather.13.cloned.1.call-start = ((), (), s32[]{:S(2)}) async-start(), calls=%async_computation.6 | async-start | bytes 4718592 | tf_op jit(solution)/shard_map/all_gather | solution.py:14
  8.7 261.7 %all-gather.17.cloned.1.call-start = ((), (), s32[]{:S(2)}) async-start(), calls=%async_computation.12 | async-start | bytes 2621440 | tf_op jit(solution)/shard_map/all_gather | solution.py:27
  195.8 149.5 %reduce-scatter.5.cloned.1.call-start = ((), (), s32[]{:S(2)}) async-start(), calls=%async_computation.7 | async-start | bytes 2621440 | tf_op jit(solution)/shard_map/reduce_scatter | solution.py:43
  270.5 17.0 %copy-start = (f32[2048,1024]{0,1:T(8,128)S(1)}, f32[2048,1024]{0,1:T(8,128)}, u32[]{:S(2)}) copy-start(f32[2048,1024]{0,1:T(8,128)} %copy.7) | copy-start | bytes 25165828
  270.5 17.0 %copy-start.1 = (f32[512,2048]{1,0:T(8,128)S(1)}, f32[512,2048]{1,0:T(8,128)}, u32[]{:S(2)}) copy-start(f32[512,2048]{1,0:T(8,128)} %all-gather.13.cloned.1.call-done) | copy-start | bytes 12582916
  302.8 91.3 %copy-start.3 = (f32[1,128,256]{2,1,0:T(8,128)S(1)}, f32[1,128,256]{2,1,0:T(8,128)}, u32[]{:S(2)}) copy-start(f32[1,128,256]{2,1,0:T(8,128)} %param.6) | copy-start | bytes 393220
  302.8 91.3 %copy-start.5 = (f32[256]{0:T(256)S(1)}, f32[256]{0:T(256)}, u32[]{:S(2)}) copy-start(f32[256]{0:T(256)} %param.8) | copy-start | bytes 3076
  302.8 91.3 %copy-start.6 = (f32[128]{0:T(128)S(1)}, f32[128]{0:T(128)}, u32[]{:S(2)}) copy-start(f32[128]{0:T(128)} %param.7) | copy-start | bytes 1540
  302.8 91.3 %reduce-scatter.7.cloned.1.call-start = ((), (), s32[]{:S(2)}) async-start(), calls=%async_computation.8 | async-start | bytes 1179648 | tf_op jit(solution)/shard_map/reduce_scatter | solution.py:44
  358.8 60.7 %all-gather.15.cloned.1.call-start = ((), (), s32[]{:S(2)}) async-start(), calls=%async_computation.9 | async-start | bytes 1179648 | tf_op jit(solution)/shard_map/all_gather | solution.py:19
  395.8 78.7 %all-gather.19.cloned.1.call-start = ((), (), s32[]{:S(2)}) async-start(), calls=%async_computation.13 | async-start | bytes 2621440 | tf_op jit(solution)/shard_map/all_gather | solution.py:27
  428.7 122.7 %reduce-scatter.9.cloned.1.call-start = ((), (), s32[]{:S(2)}) async-start(), calls=%async_computation.10 | async-start | bytes 2621440 | tf_op jit(solution)/shard_map/reduce_scatter | solution.py:43
  474.5 17.0 %copy-start.2 = (f32[512,2048]{1,0:T(8,128)S(1)}, f32[512,2048]{1,0:T(8,128)}, u32[]{:S(2)}) copy-start(f32[512,2048]{1,0:T(8,128)} %all-gather.13.cloned.1.call-done) | copy-start | bytes 12582916
  508.7 91.4 %copy-start.4 = (f32[1,128,256]{2,1,0:T(8,128)S(1)}, f32[1,128,256]{2,1,0:T(8,128)}, u32[]{:S(2)}) copy-start(f32[1,128,256]{2,1,0:T(8,128)} %reduce-scatter.7.cloned.1.call-done) | copy-start | bytes 393220
  508.7 91.4 %reduce-scatter.11.cloned.1.call-start = ((), (), s32[]{:S(2)}) async-start(), calls=%async_computation.11 | async-start | bytes 1179648 | tf_op jit(solution)/shard_map/reduce_scatter | solution.py:44
Sparse Core Ops, SparseCore 0:
  9.2 26.1 all-gather.8
  37.0 149.5 all-gather.10
  188.5 34.7 all-gather.12
  224.8 45.6 all-gather.16
  302.9 42.4 reduce-scatter.4
  358.9 35.1 reduce-scatter.6
  396.0 23.4 all-gather.14
  428.8 45.6 all-gather.18
  508.8 42.4 reduce-scatter.8
  564.9 35.1 reduce-scatter.10
where the time goes:
time: 613 us; the launch traced here: 609 us
  waiting for transfers between devices  470 us (77%)
  matrix products  112 us (18%)
  between operations  13.8 us (2%)
  local copies, waits for them, and re-layouts  9.17 us (1%)
    all_gather x1, waiting for transfers between devices, per_device(): cond_whole = lax.all_gather(cond_orbitals, 'val', axis=0, tiled=True)  151 us
    all_gather x2, waiting for transfers between devices, per_device(): pair_all = lax.all_gather(pair, 'val', axis=1, tiled=True)  92.5 us
    reduce_scatter x2, waiting for transfers between devices, per_device(): back = lax.psum_scatter(back_terms, 'val', scatter_dimension=1, tiled=True)  84.7 us
    reduce_scatter x2, waiting for transfers between devices, per_device(): lax.psum_scatter(jnp.einsum('bvn,cn->bvc', back, cond_whole, precision=hi...  70.5 us
    all_gather x2, waiting for transfers between devices, per_device(): direct_full_x = lax.all_gather(newer, 'pts', axis=2, tiled=True)  50.3 us
    dot_general x2, matrix products, per_device(): jnp.einsum('vm,bvn->bmn', val_whole, pair_all, precision=highest, preferr...  33.9 us
    dot_general x2, matrix products, per_device(): jnp.einsum('vm,bmn->bvn', val_whole, weighted, precision=highest, preferr...  32.6 us
    dot_general x2, matrix products, per_device(): jnp.einsum('bvn,cn->bvc', back, cond_whole, precision=highest, preferred_...  26.8 us
  transfers between devices with their start and end apart: 10, of which 10 were waited for; matrix products, arithmetic and copies ran while one was open for 3% of the time, Pallas kernels for 0%

commit v1 on v0

--- a/solution.py
+++ b/solution.py
@@ -24,14 +24,41 @@
             precision=highest,
             preferred_element_type=jnp.float32,
         )
-        pair_all = lax.all_gather(pair, "val", axis=1, tiled=True)
-        mixed = jnp.einsum(
+        peers, index, extent = (lax.axis_size("val"), lax.axis_index("val"), pair.shape[1])
+        right = [(i, (i + 1) % peers) for i in range(peers)]
+        behind = [(i, (i - 1) % peers) for i in range(peers)]
+        middle = peers // 2
+        from_left = from_right = pair
+        so_far = jnp.einsum(
             "vm,bvn->bmn",
-            val_whole,
-            pair_all,
+            lax.dynamic_slice_in_dim(val_whole, index * extent, pair.shape[1], axis=0),
+            pair,
             precision=highest,
             preferred_element_type=jnp.float32,
         )
+        for hop in range(1, middle + 1):
+            from_left = lax.ppermute(from_left, "val", right)
+            if hop < peers - middle:
+                from_right = lax.ppermute(from_right, "val", behind)
+                so_far = so_far + jnp.einsum(
+                    "vm,bvn->bmn",
+                    lax.dynamic_slice_in_dim(
+                        val_whole, (index + hop) % peers * extent, from_right.shape[1], axis=0
+                    ),
+                    from_right,
+                    precision=highest,
+                    preferred_element_type=jnp.float32,
+                )
+            so_far = so_far + jnp.einsum(
+                "vm,bvn->bmn",
+                lax.dynamic_slice_in_dim(
+                    val_whole, (index - hop) % peers * extent, from_left.shape[1], axis=0
+                ),
+                from_left,
+                precision=highest,
+                preferred_element_type=jnp.float32,
+            )
+        mixed = so_far
         weighted = mixed * screened[None, :, :]
         back_terms = jnp.einsum(
             "vm,bmn->bvn",

time: 613 us -> 586 us (0.956)
  waiting for transfers between devices: 470 us -> 382 us
  matrix products: 112 us -> 162 us
  starting transfers between devices: 1.33 us -> 9.61 us
    all_gather x2 -> x0, waiting for transfers between devices: 92.5 us -> none  [per_device(): pair_all = lax.all_gather(pair, 'val', axis=1, tiled=True)]
    dot_general x2 -> x8, matrix products: 33.9 us -> 73.7 us  [the longest x4 36.3 us: per_device(): jnp.einsum('vm,bvn->bmn', lax.dynamic_slice_in_dim(val_whole, (index - ho...]
    dot_general x2, matrix products: 32.6 us -> 46.1 us  [per_device(): jnp.einsum('vm,bmn->bvn', val_whole, weighted, precision=highest, preferr...]
    ppermute x0 -> x6, starting transfers between devices: none -> 9.33 us  [the longest x2 6.09 us: per_device(): from_right = lax.ppermute(from_right, 'val', behind)]
    ppermute x0 -> x6, waiting for transfers between devices: none -> 7.29 us  [the longest x4 6.43 us: per_device(): from_left = lax.ppermute(from_left, 'val', right)]
  transfers between devices with their start and end apart: 10 -> 14, of which waited for: 10 -> 11; matrix products, arithmetic and copies ran while one was open for 3% -> 12% of each run, Pallas kernels for 0% -> 0%
where the time goes in v1:
time: 586 us; the launch traced here: 580 us
  waiting for transfers between devices  382 us (65%)
  matrix products  162 us (28%)
  between operations  13.8 us (2%)
  starting transfers between devices  9.61 us (2%)
  local copies, waits for them, and re-layouts  9.38 us (2%)
    all_gather x1, waiting for transfers between devices, per_device(): cond_whole = lax.all_gather(cond_orbitals, 'val', axis=0, tiled=True)  151 us
    reduce_scatter x2, waiting for transfers between devices, per_device(): back = lax.psum_scatter(back_terms, 'val', scatter_dimension=1, tiled=True)  84.7 us
    reduce_scatter x2, waiting for transfers between devices, per_device(): lax.psum_scatter(jnp.einsum('bvn,cn->bvc', back, cond_whole, precision=hi...  70.6 us
    all_gather x2, waiting for transfers between devices, per_device(): direct_full_x = lax.all_gather(newer, 'pts', axis=2, tiled=True)  50.2 us
    dot_general x2, matrix products, per_device(): jnp.einsum('vm,bmn->bvn', val_whole, weighted, precision=highest, preferr...  46.1 us
    dot_general x4, matrix products, per_device(): jnp.einsum('vm,bvn->bmn', lax.dynamic_slice_in_dim(val_whole, (index - ho...  36.3 us
    dot_general x2, matrix products, per_device(): jnp.einsum('bvn,cn->bvc', back, cond_whole, precision=highest, preferred_...  26.8 us
    dot_general x2, matrix products, per_device(): jnp.einsum('vm,bvn->bmn', lax.dynamic_slice_in_dim(val_whole, index * ext...  19.3 us
  transfers between devices with their start and end apart: 14, of which 11 were waited for; matrix products, arithmetic and copies ran while one was open for 12% of the time, Pallas kernels for 0%

profile of v1, /device:TPU:0, one launch (start us, length us, event | category | flops | bytes accessed | tf_op | source)
XLA Modules:
  0.0 580.3 jit_solution(9048624216514535920)
XLA Ops:
  6.5 0.7 all-gather.5.cloned.1.call-update
  7.3 0.0 all-gather.7.cloned.1.call-start
  7.3 0.7 all-gather.7.cloned.1.call-update
  8.0 0.0 all-gather.9.cloned.1.call-start
  8.1 0.7 all-gather.9.cloned.1.call-update
  8.7 0.0 reduce-scatter.5.cloned.1.call-start
  8.8 26.7 %all-gather.5.cloned.1.call-done = f32[1,128,2048]{2,1,0:T(8,128)} async-done(((f32[1,128,256]{2,1,0:T(8,128)}), f32[1,128,2048]{2,1,0:T(8,128)}) %all-gather.5.cloned.1.call-update) | async-done | bytes 1048592 | tf_op jit(solution)/shard_map/all_gather | solution.py:19
  35.4 151.2 %all-gather.7.cloned.1.call-done = f32[2048,1024]{1,0:T(8,128)} async-done(((f32[512,1024]{1,0:T(8,128)}), f32[2048,1024]{1,0:T(8,128)}) %all-gather.7.cloned.1.call-update) | async-done | bytes 8388624 | tf_op jit(solution)/shard_map/all_gather | solution.py:13
  186.7 7.5 %fusion.22 = f32[128,1024]{1,0:T(8,128)S(1)} fusion(f32[2048,1024]{1,0:T(8,128)} %all-gather.7.cloned.1.call-done, f32[1,128,2048]{2,1,0:T(8,128)} %all-gather.5.cloned.1.call-done), kind=kOutput, calls=%fused_computation.20 | convolution fusion | flops 3221225472 | bytes 9961472 | tf_op jit(solution)/shard_map/bvc,cn->bvn/dot_general | solution.py:20
  194.2 0.1 collective-permute-start.1
  194.3 9.4 %copy.7 = f32[2048,1024]{0,1:T(8,128)} copy(f32[2048,1024]{1,0:T(8,128)} %param.11) | data formatting | bytes 16777216 | tf_op args[5]
  203.6 3.7 collective-permute-start
  207.4 16.0 %all-gather.9.cloned.1.call-done = f32[512,2048]{1,0:T(8,128)} async-done(((f32[64,2048]{1,0:T(8,128)}), f32[512,2048]{1,0:T(8,128)}) %all-gather.9.cloned.1.call-update) | async-done | bytes 4194320 | tf_op jit(solution)/shard_map/all_gather | solution.py:14
  223.3 10.2 %fusion.38 = f32[1024,2048]{1,0:T(8,128)} fusion(f32[128,1024]{1,0:T(8,128)S(1)} %fusion.22, f32[512,2048]{1,0:T(8,128)} %all-gather.9.cloned.1.call-done, s32[]{:T(128)S(6)} %select_n.37), kind=kOutput, calls=%fused_computation.36 | convolution fusion | flops 3221225472 | bytes 9961476 | tf_op jit(solution)/shard_map/vm,bvn->bmn/dot_general | solution.py:32
  233.6 1.6 collective-permute-start.2
  235.2 9.0 %fusion.30 = f32[1024,2048]{1,0:T(8,128)} fusion(f32[512,2048]{1,0:T(8,128)S(1)} %copy-done, s32[]{:T(128)S(6)} %select_n.41, f32[1,128,1024]{2,1,0:T(8,128)S(1)} %collective-permute-done.1), kind=kOutput, calls=%fused_computation.28 | convolution fusion | flops 3221225472 | bytes 9961476 | tf_op jit(solution)/shard_map/vm,bvn->bmn/dot_general | solution.py:52
  244.3 9.0 %fusion.34 = f32[1024,2048]{1,0:T(8,128)} fusion(f32[512,2048]{1,0:T(8,128)S(1)} %copy-done, s32[]{:T(128)S(6)} %select_n.39, f32[1,128,1024]{2,1,0:T(8,128)S(1)} %collective-permute-done), kind=kOutput, calls=%fused_computation.32 | convolution fusion | flops 3221225472 | bytes 9961476 | tf_op jit(solution)/shard_map/vm,bvn->bmn/dot_general | solution.py:43
  253.3 9.1 %fusion.26 = f32[1024,2048]{1,0:T(8,128)} fusion(f32[512,2048]{1,0:T(8,128)S(1)} %copy-done, s32[]{:T(128)S(6)} %select_n.43, f32[1,128,1024]{2,1,0:T(8,128)S(1)} %collective-permute-done.2), kind=kOutput, calls=%fused_computation.24 | convolution fusion | flops 3221225472 | bytes 9961476 | tf_op jit(solution)/shard_map/vm,bvn->bmn/dot_general | solution.py:52
  262.4 23.1 %fusion.14 = f32[1,512,1024]{1,2,0:T(8,128)} fusion(f32[512,2048]{1,0:T(8,128)} %all-gather.9.cloned.1.call-done, f32[2048,1024]{0,1:T(8,128)} %copy.7, f32[1024,2048]{1,0:T(8,128)} %fusion.26, f32[1024,2048]{1,0:T(8,128)} %fusion.30, f32[1024,2048]{1,0:T(8,128)} %fusion.38, f32[1024,2048]{1,0:T(8,128)} %fusion.34), kind=kOutput, calls=%fused_computation.16 | convolution fusion | flops 12893290496 | bytes 48234496 | tf_op jit(solution)/shard_map/vm,bmn->bvn/dot_general | solution.py:63
  285.6 0.0 reduce-scatter.5.cloned.1.call-update
  285.6 0.0 reduce-scatter.7.cloned.1.call-start
  285.6 42.8 %reduce-scatter.5.cloned.1.call-done = f32[1,128,1024]{1,2,0:T(8,128)} async-done(((f32[1,512,1024]{1,2,0:T(8,128)}), f32[1,128,1024]{1,2,0:T(8,128)}) %reduce-scatter.5.cloned.1.call-update) | async-done | bytes 524304 | tf_op jit(solution)/shard_map/reduce_scatter | solution.py:70
  328.4 13.4 %convolution_bitcast_fusion.1 = f32[1,128,2048]{2,1,0:T(8,128)} fusion(f32[2048,1024]{1,0:T(8,128)} %all-gather.7.cloned.1.call-done, f32[1,128,1024]{1,2,0:T(8,128)} %reduce-scatter.5.cloned.1.call-done), kind=kOutput, calls=%fused_computation.15 | convolution fusion | flops 3221225472 | bytes 9961472 | tf_op jit(solution)/shard_map/bvn,cn->bvc/dot_general | solution.py:72
  341.8 0.0 reduce-scatter.7.cloned.1.call-update
  341.8 0.0 all-gather.11.cloned.1.call-start
  341.9 35.3 %reduce-scatter.7.cloned.1.call-done = f32[1,128,256]{2,1,0:T(8,128)} async-done(((f32[1,128,2048]{2,1,0:T(8,128)}), f32[1,128,256]{2,1,0:T(8,128)}) %reduce-scatter.7.cloned.1.call-update) | async-done | bytes 131088 | tf_op jit(solution)/shard_map/reduce_scatter | solution.py:71
  377.2 1.7 fusion.53
  378.8 0.0 all-gather.11.cloned.1.call-update
  378.9 0.0 reduce-scatter.9.cloned.1.call-start
  378.9 23.6 %all-gather.11.cloned.1.call-done = f32[1,128,2048]{2,1,0:T(8,128)} async-done(((f32[1,128,256]{2,1,0:T(8,128)}), f32[1,128,2048]{2,1,0:T(8,128)}) %all-gather.11.cloned.1.call-update) | async-done | bytes 1048592 | tf_op jit(solution)/shard_map/all_gather | solution.py:19
  402.5 7.8 %fusion.20 = f32[128,1024]{1,0:T(8,128)S(1)} fusion(f32[2048,1024]{1,0:T(8,128)} %all-gather.7.cloned.1.call-done, f32[1,128,2048]{2,1,0:T(8,128)} %all-gather.11.cloned.1.call-done), kind=kOutput, calls=%fused_computation.18 | convolution fusion | flops 3221225472 | bytes 9961472 | tf_op jit(solution)/shard_map/bvc,cn->bvn/dot_general | solution.py:20
  410.3 1.5 collective-permute-start.4
  411.8 2.3 collective-permute-start.3
  414.2 9.1 %fusion.36 = f32[1024,2048]{1,0:T(8,128)} fusion(f32[128,1024]{1,0:T(8,128)S(1)} %fusion.20, f32[512,2048]{1,0:T(8,128)S(1)} %copy-done.1, s32[]{:T(128)S(6)} %select_n.37), kind=kOutput, calls=%fused_computation.34 | convolution fusion | flops 3221225472 | bytes 9961476 | tf_op jit(solution)/shard_map/vm,bvn->bmn/dot_general | solution.py:32
  423.3 3.7 collective-permute-done.4
  427.0 9.1 %fusion.28 = f32[1024,2048]{1,0:T(8,128)} fusion(f32[512,2048]{1,0:T(8,128)S(1)} %copy-done.1, s32[]{:T(128)S(6)} %select_n.41, f32[1,128,1024]{2,1,0:T(8,128)S(1)} %collective-permute-done.4), kind=kOutput, calls=%fused_computation.26 | convolution fusion | flops 3221225472 | bytes 9961476 | tf_op jit(solution)/shard_map/vm,bvn->bmn/dot_general | solution.py:52
  436.1 0.9 collective-permute-done.3
  436.9 9.1 %fusion.32 = f32[1024,2048]{1,0:T(8,128)} fusion(f32[512,2048]{1,0:T(8,128)S(1)} %copy-done.1, s32[]{:T(128)S(6)} %select_n.39, f32[1,128,1024]{2,1,0:T(8,128)S(1)} %collective-permute-done.3), kind=kOutput, calls=%fused_computation.30 | convolution fusion | flops 3221225472 | bytes 9961476 | tf_op jit(solution)/shard_map/vm,bvn->bmn/dot_general | solution.py:43
  446.0 2.7 collective-permute-done.5
  448.7 9.1 %fusion.24 = f32[1024,2048]{1,0:T(8,128)} fusion(f32[512,2048]{1,0:T(8,128)S(1)} %copy-done.1, s32[]{:T(128)S(6)} %select_n.43, f32[1,128,1024]{2,1,0:T(8,128)S(1)} %collective-permute-done.5), kind=kOutput, calls=%fused_computation.22 | convolution fusion | flops 3221225472 | bytes 9961476 | tf_op jit(solution)/shard_map/vm,bvn->bmn/dot_general | solution.py:52
  457.8 23.0 %fusion.17 = f32[1,512,1024]{1,2,0:T(8,128)} fusion(f32[512,2048]{1,0:T(8,128)} %all-gather.9.cloned.1.call-done, f32[2048,1024]{0,1:T(8,128)} %copy.7, f32[1024,2048]{1,0:T(8,128)} %fusion.24, f32[1024,2048]{1,0:T(8,128)} %fusion.28, f32[1024,2048]{1,0:T(8,128)} %fusion.36, f32[1024,2048]{1,0:T(8,128)} %fusion.32), kind=kOutput, calls=%fused_computation.17 | convolution fusion | flops 12893290496 | bytes 48234496 | tf_op jit(solution)/shard_map/vm,bmn->bvn/dot_general | solution.py:63
  480.8 0.0 reduce-scatter.9.cloned.1.call-update
  480.8 0.0 reduce-scatter.11.cloned.1.call-start
  480.9 41.9 %reduce-scatter.9.cloned.1.call-done = f32[1,128,1024]{1,2,0:T(8,128)} async-done(((f32[1,512,1024]{1,2,0:T(8,128)}), f32[1,128,1024]{1,2,0:T(8,128)}) %reduce-scatter.9.cloned.1.call-update) | async-done | bytes 524304 | tf_op jit(solution)/shard_map/reduce_scatter | solution.py:70
  522.7 13.4 %convolution_bitcast_fusion = f32[1,128,2048]{2,1,0:T(8,128)} fusion(f32[2048,1024]{1,0:T(8,128)} %all-gather.7.cloned.1.call-done, f32[1,128,1024]{1,2,0:T(8,128)} %reduce-scatter.9.cloned.1.call-done), kind=kOutput, calls=%fused_computation.14 | convolution fusion | flops 3221225472 | bytes 9961472 | tf_op jit(solution)/shard_map/bvn,cn->bvc/dot_general | solution.py:72
  536.1 0.0 reduce-scatter.11.cloned.1.call-update
  536.2 35.3 %reduce-scatter.11.cloned.1.call-done = f32[1,128,256]{2,1,0:T(8,128)} async-done(((f32[1,128,2048]{2,1,0:T(8,128)}), f32[1,128,256]{2,1,0:T(8,128)}) %reduce-scatter.11.cloned.1.call-update) | async-done | bytes 131088 | tf_op jit(solution)/shard_map/reduce_scatter | solution.py:71
  571.5 1.7 fusion.52
  (17 shorter events, 0.0 us)
Async XLA Ops:
  6.5 28.9 %all-gather.5.cloned.1.call-start = ((), (), s32[]{:S(2)}) async-start(), calls=%async_computation.4 | async-start | bytes 1179648 | tf_op jit(solution)/shard_map/all_gather | solution.py:19
  7.3 179.4 %all-gather.7.cloned.1.call-start = ((), (), s32[]{:S(2)}) async-start(), calls=%async_computation.5 | async-start | bytes 10485760 | tf_op jit(solution)/shard_map/all_gather | solution.py:13
  8.0 215.3 %all-gather.9.cloned.1.call-start = ((), (), s32[]{:S(2)}) async-start(), calls=%async_computation.6 | async-start | bytes 4718592 | tf_op jit(solution)/shard_map/all_gather | solution.py:14
  8.7 319.7 %reduce-scatter.5.cloned.1.call-start = ((), (), s32[]{:S(2)}) async-start(), calls=%async_computation.7 | async-start | bytes 2621440 | tf_op jit(solution)/shard_map/reduce_scatter | solution.py:70
  194.2 39.4 %collective-permute-start.1 = (f32[1,128,1024]{2,1,0:T(8,128)S(1)}, f32[1,128,1024]{2,1,0:T(8,128)S(1)}, u32[]{:S(2)}, u32[]{:S(2)}) collective-permute-start(f32[1,128,1024]{2,1,0:T(8,128)S(1)} %bitcast.93), channel_id=1, source_target_pairs={{0,1},{1,2},{2,3},{3,0},{4,5},{5,6},{6,7},{7,4},{8,9},{9,10},{10,1... | collective-permute-start | bytes 1572872 | tf_op jit(solution)/shard_map/ppermute | solution.py:40
  203.6 40.6 %collective-permute-start = (f32[1,128,1024]{2,1,0:T(8,128)S(1)}, f32[1,128,1024]{2,1,0:T(8,128)S(1)}, u32[]{:S(2)}, u32[]{:S(2)}) collective-permute-start(f32[1,128,1024]{2,1,0:T(8,128)S(1)} %bitcast.94), channel_id=1, source_target_pairs={{0,3},{1,0},{2,1},{3,2},{4,7},{5,4},{6,5},{7,6},{8,11},{9,8},{10,9... | collective-permute-start | bytes 1572872 | tf_op jit(solution)/shard_map/ppermute | solution.py:42
  223.3 11.9 %copy-start = (f32[512,2048]{1,0:T(8,128)S(1)}, f32[512,2048]{1,0:T(8,128)}, u32[]{:S(2)}) copy-start(f32[512,2048]{1,0:T(8,128)} %all-gather.9.cloned.1.call-done) | copy-start | bytes 12582916
  233.6 19.7 %collective-permute-start.2 = (f32[1,128,1024]{2,1,0:T(8,128)S(1)}, f32[1,128,1024]{2,1,0:T(8,128)S(1)}, u32[]{:S(2)}, u32[]{:S(2)}) collective-permute-start(f32[1,128,1024]{2,1,0:T(8,128)S(1)} %collective-permute-done.1), channel_id=1, source_target_pairs={{0,1},{1,2},{2,3},{3,0},{4,5},{5,6},{6,7},{7,4},{8,9},{9,10},{10,1... | collective-permute-start | bytes 1572872 | tf_op jit(solution)/shard_map/ppermute | solution.py:40
  285.5 91.6 %copy-start.2 = (f32[1,128,256]{2,1,0:T(8,128)S(1)}, f32[1,128,256]{2,1,0:T(8,128)}, u32[]{:S(2)}) copy-start(f32[1,128,256]{2,1,0:T(8,128)} %param.6) | copy-start | bytes 393220
  285.5 91.6 %copy-start.4 = (f32[256]{0:T(256)S(1)}, f32[256]{0:T(256)}, u32[]{:S(2)}) copy-start(f32[256]{0:T(256)} %param.8) | copy-start | bytes 3076
  285.5 91.6 %copy-start.5 = (f32[128]{0:T(128)S(1)}, f32[128]{0:T(128)}, u32[]{:S(2)}) copy-start(f32[128]{0:T(128)} %param.7) | copy-start | bytes 1540
  285.6 91.6 %reduce-scatter.7.cloned.1.call-start = ((), (), s32[]{:S(2)}) async-start(), calls=%async_computation.8 | async-start | bytes 1179648 | tf_op jit(solution)/shard_map/reduce_scatter | solution.py:71
  341.8 60.7 %all-gather.11.cloned.1.call-start = ((), (), s32[]{:S(2)}) async-start(), calls=%async_computation.9 | async-start | bytes 1179648 | tf_op jit(solution)/shard_map/all_gather | solution.py:19
  378.9 143.9 %reduce-scatter.9.cloned.1.call-start = ((), (), s32[]{:S(2)}) async-start(), calls=%async_computation.10 | async-start | bytes 2621440 | tf_op jit(solution)/shard_map/reduce_scatter | solution.py:70
  402.5 11.7 %copy-start.1 = (f32[512,2048]{1,0:T(8,128)S(1)}, f32[512,2048]{1,0:T(8,128)}, u32[]{:S(2)}) copy-start(f32[512,2048]{1,0:T(8,128)} %all-gather.9.cloned.1.call-done) | copy-start | bytes 12582916
  410.3 16.7 %collective-permute-start.4 = (f32[1,128,1024]{2,1,0:T(8,128)S(1)}, f32[1,128,1024]{2,1,0:T(8,128)S(1)}, u32[]{:S(2)}, u32[]{:S(2)}) collective-permute-start(f32[1,128,1024]{2,1,0:T(8,128)S(1)} %bitcast.95), channel_id=1, source_target_pairs={{0,1},{1,2},{2,3},{3,0},{4,5},{5,6},{6,7},{7,4},{8,9},{9,10},{10,1... | collective-permute-start | bytes 1572872 | tf_op jit(solution)/shard_map/ppermute | solution.py:40
  411.8 25.1 %collective-permute-start.3 = (f32[1,128,1024]{2,1,0:T(8,128)S(1)}, f32[1,128,1024]{2,1,0:T(8,128)S(1)}, u32[]{:S(2)}, u32[]{:S(2)}) collective-permute-start(f32[1,128,1024]{2,1,0:T(8,128)S(1)} %bitcast.96), channel_id=1, source_target_pairs={{0,3},{1,0},{2,1},{3,2},{4,7},{5,4},{6,5},{7,6},{8,11},{9,8},{10,9... | collective-permute-start | bytes 1572872 | tf_op jit(solution)/shard_map/ppermute | solution.py:42
  427.0 21.7 %collective-permute-start.5 = (f32[1,128,1024]{2,1,0:T(8,128)S(1)}, f32[1,128,1024]{2,1,0:T(8,128)S(1)}, u32[]{:S(2)}, u32[]{:S(2)}) collective-permute-start(f32[1,128,1024]{2,1,0:T(8,128)S(1)} %collective-permute-done.4), channel_id=1, source_target_pairs={{0,1},{1,2},{2,3},{3,0},{4,5},{5,6},{6,7},{7,4},{8,9},{9,10},{10,1... | collective-permute-start | bytes 1572872 | tf_op jit(solution)/shard_map/ppermute | solution.py:40
  480.8 90.7 %copy-start.3 = (f32[1,128,256]{2,1,0:T(8,128)S(1)}, f32[1,128,256]{2,1,0:T(8,128)}, u32[]{:S(2)}) copy-start(f32[1,128,256]{2,1,0:T(8,128)} %reduce-scatter.7.cloned.1.call-done) | copy-start | bytes 393220
  480.8 90.7 %reduce-scatter.11.cloned.1.call-start = ((), (), s32[]{:S(2)}) async-start(), calls=%async_computation.11 | async-start | bytes 1179648 | tf_op jit(solution)/shard_map/reduce_scatter | solution.py:71
Sparse Core Ops, SparseCore 0:
  9.2 26.1 all-gather.4
  37.0 149.5 all-gather.6
  188.5 34.7 all-gather.8
  285.7 42.6 reduce-scatter.4
  341.9 35.1 reduce-scatter.6
  379.0 23.4 all-gather.10
  480.9 41.7 reduce-scatter.8
  536.3 35.1 reduce-scatter.10
